TPU v7x, 256 devices: a whole 4x4x8 slice. The times are simulated.
256 devices in a mesh: dp: 8 (over y, core), ctx: 32 (over x, z).
Axes of the slice: x: 4, y: 4, z: 8, core: 2. Of those that a mesh axis runs over, the one named last changes fastest.
Arguments:
- features: bfloat16 [8, 4096, 1536], P('dp', 'ctx'), may hold values from -6 to 6
- short_weight: float32 [7, 1536], replicated, may hold values from -2 to 2
- long_filter: float32 [4096, 512], P('ctx'), may hold values from -4 to 4
- skip_bias: float32 [512], replicated, may hold values from 0.5 to 1.5
- cotangent: bfloat16 [8, 4096, 512], P('dp', 'ctx'), may hold values from -6 to 6
Outputs:
- layer_out: bfloat16 [8, 4096, 512], P('dp', 'ctx')
- grad_features: bfloat16 [8, 4096, 1536], P('dp', 'ctx')
- grad_short: float32 [7, 1536], replicated
- grad_filter: float32 [4096, 512], P('ctx')
- grad_skip: float32 [512], replicated
All inputs are finite; a program needn't handle non-finite values.
Results may differ from a plain program's by a relative error of at most 0.001.
Values may be sent and summed in bfloat16 or wider, within the bound.
A program may use at most 64 MiB of HBM per device.

v0:
```python
import math
import jax
import jax.numpy as jnp
from jax import lax
from jax.sharding import PartitionSpec as P

PRECISE = lax.Precision.HIGHEST


def swapped(value, axis, distance):
    mask = 2**distance
    pairs = [(source, source ^ mask) for source in range(lax.axis_size(axis))]
    return lax.ppermute(value, axis, pairs)


def shifted(value, axis, steps):
    count = lax.axis_size(axis)
    initial, last = (max(0, -steps), min(count, count - steps))
    return lax.ppermute(value, axis, [(source, source + steps) for source in range(initial, last)])


def bit_reverse(index_value, bit_count):
    reversed_value = jnp.zeros_like(index_value)
    for bit_place in range(bit_count):
        digit_now = index_value // 2**bit_place % 2
        reversed_value = reversed_value + digit_now * 2 ** (bit_count - 1 - bit_place)
    return reversed_value


def spectral_table(device, parts_count, tokens):
    bit_count = parts_count.bit_length() - 1
    coarse_freq = 2 * bit_reverse(device, bit_count) + jnp.arange(2, dtype=jnp.int32)
    total_points = 2 * parts_count * tokens
    column_index = jnp.arange(tokens, dtype=jnp.int32)
    full_freq = coarse_freq[:, None] + 2 * parts_count * column_index[None, :]
    phase_value = column_index[None, None, :] * full_freq[:, :, None] % total_points
    angle_value = phase_value.astype(jnp.float32) * (2.0 * math.pi / total_points)
    return (jnp.cos(angle_value), -jnp.sin(angle_value))


def contract(matrix, values):
    return jnp.einsum("akm,amw->akw", matrix, values, precision=PRECISE)


def contract_back(matrix, values):
    return jnp.einsum("akm,akw->amw", matrix, values, precision=PRECISE)


def local_forward(spec_real, spec_imag, table):
    table_real, table_imag = table
    out_real = contract(table_real, spec_real) - contract(table_imag, spec_imag)
    out_imag = contract(table_real, spec_imag) + contract(table_imag, spec_real)
    return (out_real, out_imag)


def local_inverse(spec_real, spec_imag, table):
    table_real, table_imag = table
    factor = 1.0 / spec_real.shape[1]
    out_real = (
        contract_back(table_real, spec_real) + contract_back(table_imag, spec_imag)
    ) * factor
    out_imag = (
        contract_back(table_real, spec_imag) - contract_back(table_imag, spec_real)
    ) * factor
    return (out_real, out_imag)


def pair_swap(stacked, bit_place):
    return swapped(stacked, "ctx", bit_place)


def pair_swap_back(stacked, bit_place):
    return swapped(stacked, "ctx", bit_place)


def section_terms(device, bit_place):
    span_size = 2**bit_place
    upper_flag = device // span_size % 2
    sign_value = (1 - 2 * upper_flag).astype(jnp.float32)
    turn_value = math.pi / span_size * (upper_flag * (device % span_size)).astype(jnp.float32)
    return (sign_value, jnp.cos(turn_value), jnp.sin(turn_value))


def butterfly_forward(signals):
    parts_count = lax.axis_size("ctx")
    device = lax.axis_index("ctx")
    bit_count = parts_count.bit_length() - 1
    angle_value = math.pi * device.astype(jnp.float32) / parts_count
    spec_real = jnp.stack([signals, signals * jnp.cos(angle_value)])
    spec_imag = jnp.stack([jnp.zeros_like(signals), -signals * jnp.sin(angle_value)])
    for bit_place in reversed(range(bit_count)):
        sign_value, cos_turn, sin_turn = section_terms(device, bit_place)
        partner = pair_swap(jnp.stack([spec_real, spec_imag]), bit_place)
        joined_real = partner[0] + sign_value * spec_real
        joined_imag = partner[1] + sign_value * spec_imag
        spec_real = joined_real * cos_turn + joined_imag * sin_turn
        spec_imag = joined_imag * cos_turn - joined_real * sin_turn
    return (spec_real, spec_imag)


def butterfly_inverse(spec_real, spec_imag):
    parts_count = lax.axis_size("ctx")
    device = lax.axis_index("ctx")
    bit_count = parts_count.bit_length() - 1
    for bit_place in range(bit_count):
        sign_value, cos_turn, sin_turn = section_terms(device, bit_place)
        turned_real = spec_real * cos_turn - spec_imag * sin_turn
        turned_imag = spec_imag * cos_turn + spec_real * sin_turn
        partner = pair_swap_back(jnp.stack([turned_real, turned_imag]), bit_place)
        spec_real = 0.5 * (partner[0] + sign_value * turned_real)
        spec_imag = 0.5 * (partner[1] + sign_value * turned_imag)
    angle_value = math.pi * device.astype(jnp.float32) / parts_count
    cos_last = jnp.cos(angle_value)
    sin_last = jnp.sin(angle_value)
    out_real = 0.5 * (spec_real[0] + spec_real[1] * cos_last - spec_imag[1] * sin_last)
    out_imag = 0.5 * (spec_imag[0] + spec_imag[1] * cos_last + spec_real[1] * sin_last)
    return (out_real, out_imag)


def per_device(features, short_weight, long_filter, skip_bias, cotangent):
    taps = short_weight.shape[0]
    token_rows = features[0]
    tokens = token_rows.shape[0]
    channels = long_filter.shape[1]
    parts_count = lax.axis_size("ctx")
    device = lax.axis_index("ctx")
    history = shifted(token_rows[tokens - (taps - 1) :], "ctx", 1)
    extended = jnp.concatenate([history, token_rows], axis=0).astype(jnp.float32)
    mixed_feats = jnp.zeros((tokens, token_rows.shape[1]), jnp.float32)
    for tap_index in range(taps):
        start_row = taps - 1 - tap_index
        mixed_feats = (
            mixed_feats + short_weight[tap_index] * extended[start_row : start_row + tokens]
        )
    query = mixed_feats[:, :channels]
    key_part = mixed_feats[:, channels : 2 * channels]
    value_part = mixed_feats[:, 2 * channels :]
    gated = key_part * value_part
    upstream = cotangent[0].astype(jnp.float32)
    dconv = upstream * query
    signals = jnp.concatenate([gated, long_filter, dconv], axis=1)
    table = spectral_table(device, parts_count, tokens)
    spec_real, spec_imag = butterfly_forward(signals)
    spec_real, spec_imag = local_forward(spec_real, spec_imag, table)
    gated_real = spec_real[..., :channels]
    gated_imag = spec_imag[..., :channels]
    filter_real = spec_real[..., channels : 2 * channels]
    filter_imag = spec_imag[..., channels : 2 * channels]
    dconv_real = spec_real[..., 2 * channels :]
    dconv_imag = spec_imag[..., 2 * channels :]
    conv_real = gated_real * filter_real - gated_imag * filter_imag
    conv_imag = gated_real * filter_imag + gated_imag * filter_real
    back_real = filter_real * dconv_real + filter_imag * dconv_imag
    back_imag = filter_real * dconv_imag - filter_imag * dconv_real
    corr_real = gated_real * dconv_real + gated_imag * dconv_imag
    corr_imag = gated_real * dconv_imag - gated_imag * dconv_real
    inverse_real = jnp.concatenate([conv_real - back_imag, corr_real], axis=-1)
    inverse_imag = jnp.concatenate([conv_imag + back_real, corr_imag], axis=-1)
    inverse_real, inverse_imag = local_inverse(inverse_real, inverse_imag, table)
    result_real, result_imag = butterfly_inverse(inverse_real, inverse_imag)
    long_conv = result_real[:, :channels] + skip_bias * gated
    dgated = result_imag[:, :channels] + skip_bias * dconv
    filter_part = result_real[:, channels:]
    layer_out = (query * long_conv).astype(jnp.bfloat16)[None]
    dmixed = jnp.concatenate([upstream * long_conv, dgated * value_part, dgated * key_part], axis=1)
    later = shifted(dmixed[: taps - 1], "ctx", -1)
    ahead = jnp.concatenate([dmixed, later], axis=0)
    grad_local = jnp.zeros_like(dmixed)
    short_rows = []
    for tap_index in range(taps):
        grad_local = grad_local + short_weight[tap_index] * ahead[tap_index : tap_index + tokens]
        start_row = taps - 1 - tap_index
        short_rows.append(jnp.sum(dmixed * extended[start_row : start_row + tokens], axis=0))
    grad_features = grad_local.astype(jnp.bfloat16)[None]
    short_part = jnp.stack(short_rows)
    skip_part = jnp.sum(dconv * gated, axis=0)
    scale = 1.0 / math.sqrt(lax.axis_size("dp") * parts_count * tokens)
    filter_sum = lax.psum(filter_part, "dp")
    short_sum, skip_sum = lax.psum((short_part, skip_part), ("dp", "ctx"))
    return (layer_out, grad_features, short_sum * scale, filter_sum * scale, skip_sum * scale)


def solution(mesh):
    return jax.shard_map(
        per_device,
        mesh=mesh,
        in_specs=(P("dp", "ctx", None), P(), P("ctx", None), P(), P("dp", "ctx", None)),
        out_specs=(P("dp", "ctx", None), P("dp", "ctx", None), P(), P("ctx", None), P()),
        check_vma=False,
    )
```

profile of v0, /device:TPU:2, one launch (start us, length us, event | category | flops | bytes accessed | tf_op | source)
XLA Modules:
  0.0 1050.0 jit_solution(7923902592177502704)
XLA Ops:
  8.0 3.8 collective-permute-start
  13.2 4.3 collective-permute-done
  26.5 68.2 %collective-permute-done.1 = f32[2,2,128,1536]{3,2,1,0:T(8,128)} collective-permute-done((f32[2,2,128,1536]{3,2,1,0:T(8,128)}, f32[2,2,128,1536]{3,2,1,0:T(8,128)}, u32[]{:S(2)}, u32[]{:S(2)}) %collective-permute-start.1) | collective-permute-done | bytes 3145760 | tf_op jit(solution)/shard_map/ppermute | solution.py:13
  94.7 3.0 multiply_subtract_fusion.4
  100.3 67.9 %collective-permute-done.2 = f32[2,2,128,1536]{3,2,1,0:T(8,128)} collective-permute-done((f32[2,2,128,1536]{3,2,1,0:T(8,128)}, f32[2,2,128,1536]{3,2,1,0:T(8,128)}, u32[]{:S(2)}, u32[]{:S(2)}) %collective-permute-start.2) | collective-permute-done | bytes 3145760 | tf_op jit(solution)/shard_map/ppermute | solution.py:13
  168.2 3.1 multiply_subtract_fusion.3
  174.0 4.0 collective-permute-start.3
  178.1 135.4 %collective-permute-done.3 = f32[2,2,128,1536]{3,2,1,0:T(8,128)} collective-permute-done((f32[2,2,128,1536]{3,2,1,0:T(8,128)}, f32[2,2,128,1536]{3,2,1,0:T(8,128)}, u32[]{:S(2)}, u32[]{:S(2)}) %collective-permute-start.3) | collective-permute-done | bytes 3145760 | tf_op jit(solution)/shard_map/ppermute | solution.py:13
  313.5 3.6 multiply_subtract_fusion.2
  319.4 137.3 %collective-permute-done.4 = f32[2,2,128,1536]{3,2,1,0:T(8,128)} collective-permute-done((f32[2,2,128,1536]{3,2,1,0:T(8,128)}, f32[2,2,128,1536]{3,2,1,0:T(8,128)}, u32[]{:S(2)}, u32[]{:S(2)}) %collective-permute-start.4) | collective-permute-done | bytes 3145760 | tf_op jit(solution)/shard_map/ppermute | solution.py:13
  456.7 3.1 multiply_add_fusion.1
  462.6 69.4 %collective-permute-done.5 = f32[2,2,128,1536]{3,2,1,0:T(8,128)} collective-permute-done((f32[2,2,128,1536]{3,2,1,0:T(8,128)}, f32[2,2,128,1536]{3,2,1,0:T(8,128)}, u32[]{:S(2)}, u32[]{:S(2)}) %collective-permute-start.5) | collective-permute-done | bytes 3145760 | tf_op jit(solution)/shard_map/ppermute | solution.py:13
  532.0 3.5 fusion.2
  552.4 45.8 %collective-permute-done.6 = f32[2,2,128,1024]{3,2,1,0:T(8,128)} collective-permute-done((f32[2,2,128,1024]{3,2,1,0:T(8,128)}, f32[2,2,128,1024]{3,2,1,0:T(8,128)}, u32[]{:S(2)}, u32[]{:S(2)}) %collective-permute-start.6) | collective-permute-done | bytes 2097184 | tf_op jit(solution)/shard_map/ppermute | solution.py:13
  604.8 89.6 %collective-permute-done.7 = f32[2,2,128,1024]{3,2,1,0:T(8,128)} collective-permute-done((f32[2,2,128,1024]{3,2,1,0:T(8,128)}, f32[2,2,128,1024]{3,2,1,0:T(8,128)}, u32[]{:S(2)}, u32[]{:S(2)}) %collective-permute-start.7) | collective-permute-done | bytes 2097184 | tf_op jit(solution)/shard_map/ppermute | solution.py:13
  698.1 3.7 collective-permute-start.8
  701.8 92.3 %collective-permute-done.8 = f32[2,2,128,1024]{3,2,1,0:T(8,128)} collective-permute-done((f32[2,2,128,1024]{3,2,1,0:T(8,128)S(1)}, f32[2,2,128,1024]{3,2,1,0:T(8,128)}, u32[]{:S(2)}, u32[]{:S(2)}) %collective-permute-start.8) | collective-permute-done | bytes 2097184 | tf_op jit(solution)/shard_map/ppermute | solution.py:13
  794.1 2.7 multiply_add_fusion.6
  799.2 46.3 %collective-permute-done.9 = f32[2,2,128,1024]{3,2,1,0:T(8,128)} collective-permute-done((f32[2,2,128,1024]{3,2,1,0:T(8,128)}, f32[2,2,128,1024]{3,2,1,0:T(8,128)}, u32[]{:S(2)}, u32[]{:S(2)}) %collective-permute-start.9) | collective-permute-done | bytes 2097184 | tf_op jit(solution)/shard_map/ppermute | solution.py:13
  847.8 3.2 collective-permute-start.10
  851.0 45.0 %collective-permute-done.10 = f32[2,2,128,1024]{3,2,1,0:T(8,128)S(1)} collective-permute-done((f32[2,2,128,1024]{3,2,1,0:T(8,128)S(1)}, f32[2,2,128,1024]{3,2,1,0:T(8,128)S(1)}, u32[]{:S(2)}, u32[]{:S(2)}) %collective-permute-start.10) | collective-permute-done | bytes 2097184 | tf_op jit(solution)/shard_map/ppermute | solution.py:13
  899.7 75.3 %all-reduce.1 = (f32[7,1536]{1,0:T(8,128)S(1)}, f32[512]{0:T(512)S(1)}) all-reduce(f32[7,1536]{1,0:T(8,128)S(1)} %stack.165, f32[512]{0:T(512)S(1)} %get-tuple-element.21), channel_id=1, replica_groups=mesh['dp'=8,'ctx'=32] {'dp','ctx'}, use_global_device_ids=true, to_apply=%region_7.8 | all-reduce | flops 11264 | bytes 90112 | tf_op jit(solution)/shard_map/psum | solution.py:179
  975.7 4.7 collective-permute-start.11
  983.7 57.8 %all-reduce.4.cloned.1.call-done = f32[128,512]{1,0:T(8,128)} async-done(((f32[128,512]{1,0:T(8,128)}), f32[128,512]{1,0:T(8,128)}) %all-reduce.4.cloned.1.call-update) | async-done | bytes 262160 | tf_op jit(solution)/shard_map/psum | solution.py:178
  (102 shorter events, 61.6 us)
Async XLA Ops:
  7.2 1034.3 %all-reduce.4.cloned.1.call-start = ((), (), s32[]{:S(2)}) async-start(), calls=%async_computation | async-start | bytes 524288 | tf_op jit(solution)/shard_map/psum | solution.py:178
  8.0 9.5 collective-permute-start
  19.5 1.4 copy-start.9
  19.6 1.3 copy-start.13
  23.9 70.8 %collective-permute-start.1 = (f32[2,2,128,1536]{3,2,1,0:T(8,128)}, f32[2,2,128,1536]{3,2,1,0:T(8,128)}, u32[]{:S(2)}, u32[]{:S(2)}) collective-permute-start(f32[2,2,128,1536]{3,2,1,0:T(8,128)} %pad_maximum_fusion), channel_id=1, source_target_pairs={{0,16},{1,17},{2,18},{3,19},{4,20},{5,21},{6,22},{7,23},{8,24},{9,... | collective-permute-start | bytes 9437192 | tf_op jit(solution)/shard_map/ppermute | solution.py:13
  97.7 2.1 copy-start.1
  99.8 68.4 %collective-permute-start.2 = (f32[2,2,128,1536]{3,2,1,0:T(8,128)}, f32[2,2,128,1536]{3,2,1,0:T(8,128)}, u32[]{:S(2)}, u32[]{:S(2)}) collective-permute-start(f32[2,2,128,1536]{3,2,1,0:T(8,128)} %pad_maximum_fusion.1), channel_id=1, source_target_pairs={{0,8},{1,9},{2,10},{3,11},{4,12},{5,13},{6,14},{7,15},{8,0},{9,1},... | collective-permute-start | bytes 9437192 | tf_op jit(solution)/shard_map/ppermute | solution.py:13
  171.3 2.3 copy-start.2
  171.3 2.7 copy-start.3
  174.0 139.6 %collective-permute-start.3 = (f32[2,2,128,1536]{3,2,1,0:T(8,128)}, f32[2,2,128,1536]{3,2,1,0:T(8,128)}, u32[]{:S(2)}, u32[]{:S(2)}) collective-permute-start(f32[2,2,128,1536]{3,2,1,0:T(8,128)} %pad_maximum_fusion.2), channel_id=1, source_target_pairs={{0,4},{1,5},{2,6},{3,7},{4,0},{5,1},{6,2},{7,3},{8,12},{9,13},{10,... | collective-permute-start | bytes 9437192 | tf_op jit(solution)/shard_map/ppermute | solution.py:13
  317.1 2.1 copy-start
  319.3 137.4 %collective-permute-start.4 = (f32[2,2,128,1536]{3,2,1,0:T(8,128)}, f32[2,2,128,1536]{3,2,1,0:T(8,128)}, u32[]{:S(2)}, u32[]{:S(2)}) collective-permute-start(f32[2,2,128,1536]{3,2,1,0:T(8,128)} %pad_maximum_fusion.3), channel_id=1, source_target_pairs={{0,2},{1,3},{2,0},{3,1},{4,6},{5,7},{6,4},{7,5},{8,10},{9,11},{10,... | collective-permute-start | bytes 9437192 | tf_op jit(solution)/shard_map/ppermute | solution.py:13
  459.8 2.1 copy-start.4
  459.8 2.7 copy-start.5
  462.5 69.5 %collective-permute-start.5 = (f32[2,2,128,1536]{3,2,1,0:T(8,128)}, f32[2,2,128,1536]{3,2,1,0:T(8,128)}, u32[]{:S(2)}, u32[]{:S(2)}) collective-permute-start(f32[2,2,128,1536]{3,2,1,0:T(8,128)} %pad_maximum_fusion.4), channel_id=1, source_target_pairs={{0,1},{1,0},{2,3},{3,2},{4,5},{5,4},{6,7},{7,6},{8,9},{9,8},{10,11... | collective-permute-start | bytes 9437192 | tf_op jit(solution)/shard_map/ppermute | solution.py:13
  552.1 46.1 %collective-permute-start.6 = (f32[2,2,128,1024]{3,2,1,0:T(8,128)}, f32[2,2,128,1024]{3,2,1,0:T(8,128)}, u32[]{:S(2)}, u32[]{:S(2)}) collective-permute-start(f32[2,2,128,1024]{3,2,1,0:T(8,128)} %pad_maximum_fusion.5), channel_id=1, source_target_pairs={{0,1},{1,0},{2,3},{3,2},{4,5},{5,4},{6,7},{7,6},{8,9},{9,8},{10,11... | collective-permute-start | bytes 6291464 | tf_op jit(solution)/shard_map/ppermute | solution.py:13
  602.7 91.7 %collective-permute-start.7 = (f32[2,2,128,1024]{3,2,1,0:T(8,128)}, f32[2,2,128,1024]{3,2,1,0:T(8,128)}, u32[]{:S(2)}, u32[]{:S(2)}) collective-permute-start(f32[2,2,128,1024]{3,2,1,0:T(8,128)} %pad_maximum_fusion.6), channel_id=1, source_target_pairs={{0,2},{1,3},{2,0},{3,1},{4,6},{5,7},{6,4},{7,5},{8,10},{9,11},{10,... | collective-permute-start | bytes 6291464 | tf_op jit(solution)/shard_map/ppermute | solution.py:13
  696.8 1.3 copy-start.8
  698.1 96.0 %collective-permute-start.8 = (f32[2,2,128,1024]{3,2,1,0:T(8,128)S(1)}, f32[2,2,128,1024]{3,2,1,0:T(8,128)}, u32[]{:S(2)}, u32[]{:S(2)}) collective-permute-start(f32[2,2,128,1024]{3,2,1,0:T(8,128)S(1)} %pad_maximum_fusion.7), channel_id=1, source_target_pairs={{0,4},{1,5},{2,6},{3,7},{4,0},{5,1},{6,2},{7,3},{8,12},{9,13},{10,... | collective-permute-start | bytes 6291464 | tf_op jit(solution)/shard_map/ppermute | solution.py:13
  798.3 47.3 %collective-permute-start.9 = (f32[2,2,128,1024]{3,2,1,0:T(8,128)}, f32[2,2,128,1024]{3,2,1,0:T(8,128)}, u32[]{:S(2)}, u32[]{:S(2)}) collective-permute-start(f32[2,2,128,1024]{3,2,1,0:T(8,128)} %pad_maximum_fusion.8), channel_id=1, source_target_pairs={{0,8},{1,9},{2,10},{3,11},{4,12},{5,13},{6,14},{7,15},{8,0},{9,1},... | collective-permute-start | bytes 6291464 | tf_op jit(solution)/shard_map/ppermute | solution.py:13
  847.8 48.2 %collective-permute-start.10 = (f32[2,2,128,1024]{3,2,1,0:T(8,128)S(1)}, f32[2,2,128,1024]{3,2,1,0:T(8,128)S(1)}, u32[]{:S(2)}, u32[]{:S(2)}) collective-permute-start(f32[2,2,128,1024]{3,2,1,0:T(8,128)S(1)} %pad_maximum_fusion.9), channel_id=1, source_target_pairs={{0,16},{1,17},{2,18},{3,19},{4,20},{5,21},{6,22},{7,23},{8,24},{9,... | collective-permute-start | bytes 6291464 | tf_op jit(solution)/shard_map/ppermute | solution.py:13
  896.6 1.2 copy-start.17
  896.7 1.2 copy-start.18
  975.7 6.5 collective-permute-start.11
  (8 other events, 8.3 us)
Sparse Core Ops, SparseCore 0:
  981.2 60.1 all-reduce.3
where the time goes:
time: 1050 us
  waiting for transfers between devices  860 us (82%)
  blocking collectives  75.3 us (7%)
  other arithmetic  50.7 us (5%)
  starting transfers between devices  25.6 us (2%)
  between operations  15.3 us (1%)
  matrix products  14.2 us (1%)
    ppermute x10, waiting for transfers between devices, swapped(): return lax.ppermute(value, axis, pairs)  797 us
    psum x1, blocking collectives, per_device(): short_sum, skip_sum = lax.psum((short_part, skip_part), ('dp', 'ctx'))  75.3 us
    psum x1, waiting for transfers between devices, per_device(): filter_sum = lax.psum(filter_part, 'dp')  57.8 us
  transfers between devices with their start and end apart: 13, of which 13 were waited for; matrix products, arithmetic and copies ran while one was open for 0% of the time, Pallas kernels for 0%

commit v1 on v0

--- a/solution.py
+++ b/solution.py
@@ -175,7 +175,11 @@
     short_part = jnp.stack(short_rows)
     skip_part = jnp.sum(dconv * gated, axis=0)
     scale = 1.0 / math.sqrt(lax.axis_size("dp") * parts_count * tokens)
-    filter_sum = lax.psum(filter_part, "dp")
+    filter_sum = filter_part
+    for hop in (1, 2, 4):
+        filter_sum = filter_sum + lax.ppermute(
+            filter_sum, "dp", [(dev, dev ^ hop) for dev in range(8)]
+        )
     short_sum, skip_sum = lax.psum((short_part, skip_part), ("dp", "ctx"))
     return (layer_out, grad_features, short_sum * scale, filter_sum * scale, skip_sum * scale)
 

time: 1050 us -> 989 us (0.942)
  waiting for transfers between devices: 860 us -> 810 us
  between operations: 15.3 us -> 1.95 us
    psum x1 -> x0, waiting for transfers between devices: 57.8 us -> none  [per_device(): filter_sum = lax.psum(filter_part, 'dp')]
  transfers between devices with their start and end apart: 13 -> 15, of which waited for: 13 -> 14; matrix products, arithmetic and copies ran while one was open for 0% -> 0% of each run, Pallas kernels for 0% -> 0%
where the time goes in v1:
time: 989 us; the launch traced here: 988 us
  waiting for transfers between devices  810 us (82%)
  blocking collectives  75.2 us (8%)
  other arithmetic  50 us (5%)
  starting transfers between devices  29.3 us (3%)
  matrix products  14.2 us (1%)
    ppermute x10, waiting for transfers between devices, swapped(): return lax.ppermute(value, axis, pairs)  797 us
    psum x1, blocking collectives, per_device(): short_sum, skip_sum = lax.psum((short_part, skip_part), ('dp', 'ctx'))  75.2 us
  transfers between devices with their start and end apart: 15, of which 14 were waited for; matrix products, arithmetic and copies ran while one was open for 0% of the time, Pallas kernels for 0%

profile of v1, /device:TPU:2, one launch (start us, length us, event | category | flops | bytes accessed | tf_op | source)
XLA Modules:
  0.0 987.9 jit_solution(6441329548320270847)
XLA Ops:
  1.4 3.8 collective-permute-start
  6.7 4.3 collective-permute-done
  19.9 68.2 %collective-permute-done.1 = f32[2,2,128,1536]{3,2,1,0:T(8,128)} collective-permute-done((f32[2,2,128,1536]{3,2,1,0:T(8,128)}, f32[2,2,128,1536]{3,2,1,0:T(8,128)}, u32[]{:S(2)}, u32[]{:S(2)}) %collective-permute-start.1) | collective-permute-done | bytes 3145760 | tf_op jit(solution)/shard_map/ppermute | solution.py:13
  88.1 3.0 multiply_subtract_fusion.4
  93.7 67.9 %collective-permute-done.2 = f32[2,2,128,1536]{3,2,1,0:T(8,128)} collective-permute-done((f32[2,2,128,1536]{3,2,1,0:T(8,128)}, f32[2,2,128,1536]{3,2,1,0:T(8,128)}, u32[]{:S(2)}, u32[]{:S(2)}) %collective-permute-start.2) | collective-permute-done | bytes 3145760 | tf_op jit(solution)/shard_map/ppermute | solution.py:13
  161.6 3.1 multiply_subtract_fusion.3
  167.4 4.0 collective-permute-start.3
  171.6 135.3 %collective-permute-done.3 = f32[2,2,128,1536]{3,2,1,0:T(8,128)} collective-permute-done((f32[2,2,128,1536]{3,2,1,0:T(8,128)}, f32[2,2,128,1536]{3,2,1,0:T(8,128)}, u32[]{:S(2)}, u32[]{:S(2)}) %collective-permute-start.3) | collective-permute-done | bytes 3145760 | tf_op jit(solution)/shard_map/ppermute | solution.py:13
  306.9 3.6 multiply_subtract_fusion.2
  312.9 137.3 %collective-permute-done.4 = f32[2,2,128,1536]{3,2,1,0:T(8,128)} collective-permute-done((f32[2,2,128,1536]{3,2,1,0:T(8,128)}, f32[2,2,128,1536]{3,2,1,0:T(8,128)}, u32[]{:S(2)}, u32[]{:S(2)}) %collective-permute-start.4) | collective-permute-done | bytes 3145760 | tf_op jit(solution)/shard_map/ppermute | solution.py:13
  450.1 3.1 multiply_add_fusion.1
  456.0 69.4 %collective-permute-done.5 = f32[2,2,128,1536]{3,2,1,0:T(8,128)} collective-permute-done((f32[2,2,128,1536]{3,2,1,0:T(8,128)}, f32[2,2,128,1536]{3,2,1,0:T(8,128)}, u32[]{:S(2)}, u32[]{:S(2)}) %collective-permute-start.5) | collective-permute-done | bytes 3145760 | tf_op jit(solution)/shard_map/ppermute | solution.py:13
  525.4 3.5 fusion.2
  545.8 45.8 %collective-permute-done.6 = f32[2,2,128,1024]{3,2,1,0:T(8,128)} collective-permute-done((f32[2,2,128,1024]{3,2,1,0:T(8,128)}, f32[2,2,128,1024]{3,2,1,0:T(8,128)}, u32[]{:S(2)}, u32[]{:S(2)}) %collective-permute-start.6) | collective-permute-done | bytes 2097184 | tf_op jit(solution)/shard_map/ppermute | solution.py:13
  598.3 89.6 %collective-permute-done.7 = f32[2,2,128,1024]{3,2,1,0:T(8,128)} collective-permute-done((f32[2,2,128,1024]{3,2,1,0:T(8,128)}, f32[2,2,128,1024]{3,2,1,0:T(8,128)}, u32[]{:S(2)}, u32[]{:S(2)}) %collective-permute-start.7) | collective-permute-done | bytes 2097184 | tf_op jit(solution)/shard_map/ppermute | solution.py:13
  691.6 3.8 collective-permute-start.8
  695.4 92.3 %collective-permute-done.8 = f32[2,2,128,1024]{3,2,1,0:T(8,128)} collective-permute-done((f32[2,2,128,1024]{3,2,1,0:T(8,128)S(1)}, f32[2,2,128,1024]{3,2,1,0:T(8,128)}, u32[]{:S(2)}, u32[]{:S(2)}) %collective-permute-start.8) | collective-permute-done | bytes 2097184 | tf_op jit(solution)/shard_map/ppermute | solution.py:13
  787.7 2.7 multiply_add_fusion.6
  792.7 46.2 %collective-permute-done.9 = f32[2,2,128,1024]{3,2,1,0:T(8,128)} collective-permute-done((f32[2,2,128,1024]{3,2,1,0:T(8,128)}, f32[2,2,128,1024]{3,2,1,0:T(8,128)}, u32[]{:S(2)}, u32[]{:S(2)}) %collective-permute-start.9) | collective-permute-done | bytes 2097184 | tf_op jit(solution)/shard_map/ppermute | solution.py:13
  841.2 3.3 collective-permute-start.10
  844.5 45.0 %collective-permute-done.10 = f32[2,2,128,1024]{3,2,1,0:T(8,128)S(1)} collective-permute-done((f32[2,2,128,1024]{3,2,1,0:T(8,128)S(1)}, f32[2,2,128,1024]{3,2,1,0:T(8,128)S(1)}, u32[]{:S(2)}, u32[]{:S(2)}) %collective-permute-start.10) | collective-permute-done | bytes 2097184 | tf_op jit(solution)/shard_map/ppermute | solution.py:13
  895.5 75.2 %all-reduce.1 = (f32[7,1536]{1,0:T(8,128)S(1)}, f32[512]{0:T(512)S(1)}) all-reduce(f32[7,1536]{1,0:T(8,128)S(1)} %stack.165, f32[512]{0:T(512)S(1)} %get-tuple-element.21), channel_id=1, replica_groups=mesh['dp'=8,'ctx'=32] {'dp','ctx'}, use_global_device_ids=true, to_apply=%region_7.8 | all-reduce | flops 11264 | bytes 90112 | tf_op jit(solution)/shard_map/psum | solution.py:183
  971.4 5.1 collective-permute-start.11
  981.3 5.9 collective-permute-done.14
  (107 shorter events, 64.6 us)
Async XLA Ops:
  1.4 9.5 collective-permute-start
  17.3 70.8 %collective-permute-start.1 = (f32[2,2,128,1536]{3,2,1,0:T(8,128)}, f32[2,2,128,1536]{3,2,1,0:T(8,128)}, u32[]{:S(2)}, u32[]{:S(2)}) collective-permute-start(f32[2,2,128,1536]{3,2,1,0:T(8,128)} %pad_maximum_fusion), channel_id=1, source_target_pairs={{0,16},{1,17},{2,18},{3,19},{4,20},{5,21},{6,22},{7,23},{8,24},{9,... | collective-permute-start | bytes 9437192 | tf_op jit(solution)/shard_map/ppermute | solution.py:13
  91.1 2.1 copy-start.1
  93.3 68.4 %collective-permute-start.2 = (f32[2,2,128,1536]{3,2,1,0:T(8,128)}, f32[2,2,128,1536]{3,2,1,0:T(8,128)}, u32[]{:S(2)}, u32[]{:S(2)}) collective-permute-start(f32[2,2,128,1536]{3,2,1,0:T(8,128)} %pad_maximum_fusion.1), channel_id=1, source_target_pairs={{0,8},{1,9},{2,10},{3,11},{4,12},{5,13},{6,14},{7,15},{8,0},{9,1},... | collective-permute-start | bytes 9437192 | tf_op jit(solution)/shard_map/ppermute | solution.py:13
  164.7 2.3 copy-start.2
  164.7 2.7 copy-start.3
  167.4 139.5 %collective-permute-start.3 = (f32[2,2,128,1536]{3,2,1,0:T(8,128)}, f32[2,2,128,1536]{3,2,1,0:T(8,128)}, u32[]{:S(2)}, u32[]{:S(2)}) collective-permute-start(f32[2,2,128,1536]{3,2,1,0:T(8,128)} %pad_maximum_fusion.2), channel_id=1, source_target_pairs={{0,4},{1,5},{2,6},{3,7},{4,0},{5,1},{6,2},{7,3},{8,12},{9,13},{10,... | collective-permute-start | bytes 9437192 | tf_op jit(solution)/shard_map/ppermute | solution.py:13
  310.6 2.1 copy-start
  312.7 137.4 %collective-permute-start.4 = (f32[2,2,128,1536]{3,2,1,0:T(8,128)}, f32[2,2,128,1536]{3,2,1,0:T(8,128)}, u32[]{:S(2)}, u32[]{:S(2)}) collective-permute-start(f32[2,2,128,1536]{3,2,1,0:T(8,128)} %pad_maximum_fusion.3), channel_id=1, source_target_pairs={{0,2},{1,3},{2,0},{3,1},{4,6},{5,7},{6,4},{7,5},{8,10},{9,11},{10,... | collective-permute-start | bytes 9437192 | tf_op jit(solution)/shard_map/ppermute | solution.py:13
  453.2 2.1 copy-start.4
  453.2 2.7 copy-start.5
  455.9 69.5 %collective-permute-start.5 = (f32[2,2,128,1536]{3,2,1,0:T(8,128)}, f32[2,2,128,1536]{3,2,1,0:T(8,128)}, u32[]{:S(2)}, u32[]{:S(2)}) collective-permute-start(f32[2,2,128,1536]{3,2,1,0:T(8,128)} %pad_maximum_fusion.4), channel_id=1, source_target_pairs={{0,1},{1,0},{2,3},{3,2},{4,5},{5,4},{6,7},{7,6},{8,9},{9,8},{10,11... | collective-permute-start | bytes 9437192 | tf_op jit(solution)/shard_map/ppermute | solution.py:13
  545.5 46.1 %collective-permute-start.6 = (f32[2,2,128,1024]{3,2,1,0:T(8,128)}, f32[2,2,128,1024]{3,2,1,0:T(8,128)}, u32[]{:S(2)}, u32[]{:S(2)}) collective-permute-start(f32[2,2,128,1024]{3,2,1,0:T(8,128)} %pad_maximum_fusion.5), channel_id=1, source_target_pairs={{0,1},{1,0},{2,3},{3,2},{4,5},{5,4},{6,7},{7,6},{8,9},{9,8},{10,11... | collective-permute-start | bytes 6291464 | tf_op jit(solution)/shard_map/ppermute | solution.py:13
  596.1 91.8 %collective-permute-start.7 = (f32[2,2,128,1024]{3,2,1,0:T(8,128)}, f32[2,2,128,1024]{3,2,1,0:T(8,128)}, u32[]{:S(2)}, u32[]{:S(2)}) collective-permute-start(f32[2,2,128,1024]{3,2,1,0:T(8,128)} %pad_maximum_fusion.6), channel_id=1, source_target_pairs={{0,2},{1,3},{2,0},{3,1},{4,6},{5,7},{6,4},{7,5},{8,10},{9,11},{10,... | collective-permute-start | bytes 6291464 | tf_op jit(solution)/shard_map/ppermute | solution.py:13
  691.6 96.1 %collective-permute-start.8 = (f32[2,2,128,1024]{3,2,1,0:T(8,128)S(1)}, f32[2,2,128,1024]{3,2,1,0:T(8,128)}, u32[]{:S(2)}, u32[]{:S(2)}) collective-permute-start(f32[2,2,128,1024]{3,2,1,0:T(8,128)S(1)} %pad_maximum_fusion.7), channel_id=1, source_target_pairs={{0,4},{1,5},{2,6},{3,7},{4,0},{5,1},{6,2},{7,3},{8,12},{9,13},{10,... | collective-permute-start | bytes 6291464 | tf_op jit(solution)/shard_map/ppermute | solution.py:13
  791.8 47.1 %collective-permute-start.9 = (f32[2,2,128,1024]{3,2,1,0:T(8,128)}, f32[2,2,128,1024]{3,2,1,0:T(8,128)}, u32[]{:S(2)}, u32[]{:S(2)}) collective-permute-start(f32[2,2,128,1024]{3,2,1,0:T(8,128)} %pad_maximum_fusion.8), channel_id=1, source_target_pairs={{0,8},{1,9},{2,10},{3,11},{4,12},{5,13},{6,14},{7,15},{8,0},{9,1},... | collective-permute-start | bytes 6291464 | tf_op jit(solution)/shard_map/ppermute | solution.py:13
  841.2 48.3 %collective-permute-start.10 = (f32[2,2,128,1024]{3,2,1,0:T(8,128)S(1)}, f32[2,2,128,1024]{3,2,1,0:T(8,128)S(1)}, u32[]{:S(2)}, u32[]{:S(2)}) collective-permute-start(f32[2,2,128,1024]{3,2,1,0:T(8,128)S(1)} %pad_maximum_fusion.9), channel_id=1, source_target_pairs={{0,16},{1,17},{2,18},{3,19},{4,20},{5,21},{6,22},{7,23},{8,24},{9,... | collective-permute-start | bytes 6291464 | tf_op jit(solution)/shard_map/ppermute | solution.py:13
  890.2 1.9 copy-start.10
  890.2 1.9 copy-start.14
  890.2 1.9 copy-start.17
  890.5 1.6 collective-permute-start.12
  893.0 85.3 %collective-permute-start.13 = (f32[128,512]{1,0:T(8,128)S(1)}, f32[128,512]{1,0:T(8,128)S(1)}, u32[]{:S(2)}, u32[]{:S(2)}) collective-permute-start(f32[128,512]{1,0:T(8,128)S(1)} %get-tuple-element.64), channel_id=1, source_target_pairs={{0,64},{32,96},{64,0},{96,32},{128,192},{160,224},{192,128},{224,1... | collective-permute-start | bytes 786440 | tf_op jit(solution)/shard_map/ppermute | solution.py:180
  971.4 6.9 collective-permute-start.11
  978.4 8.8 collective-permute-start.14
  (10 other events, 11.8 us)
